TPU v7x, 256 devices: a whole 4x4x8 slice. The times are simulated.
256 devices in a mesh: row: 8 (over x_hi, y), col: 32 (over z, x_lo, core).
Axes of the slice: x: 4 (x_hi: 2, x_lo: 2; x = x_hi * 2 + x_lo), y: 4, z: 8, core: 2. Of those that a mesh axis runs over, the one named last changes fastest.
Arguments:
- feats: bfloat16 [32, 1024, 512], P('col', 'row'), may hold values from -6 to 6
- weight: bfloat16 [512, 512], replicated, may hold values from -0.25 to 0.25
- cotangent: bfloat16 [8, 4096, 512], P('row', 'col'), may hold values from -6 to 6
- tile_values: bfloat16 [8, 32, 96, 128, 128], P('row', 'col'), may hold values from -0.078125 to 0.078125
- tile_rows: int32 [8, 32, 96], P('row', 'col'), may hold values from 0 to 31, as said below
- tile_cols: int32 [8, 32, 96], P('row', 'col'), may hold values from 0 to 7, as said below
- tile_count: int32 [8, 32], P('row', 'col'), may hold values from 1 to 96, as said below
Outputs:
- layer_out: bfloat16 [8, 4096, 512], P('row', 'col')
- feat_grad: bfloat16 [32, 1024, 512], P('col', 'row')
- weight_grad: float32 [512, 512], replicated
Inputs may be any that keep to these rules, and one draw needn't show every extreme that they name: `tile_rows`: with tile_cols, the tile coordinates of each block's listed tiles; no tile appears twice in a block's list. `tile_cols`: with tile_rows, the tile coordinates of each block's listed tiles. `tile_count`: slots at or beyond a block's count are unused; some block lists exactly 96 tiles.
All inputs are finite; a program needn't handle non-finite values.
Results may differ from a plain program's by a relative error of at most 0.024.
Values may be sent and summed in bfloat16 or wider, within the bound.
A program may use at most 128 MiB of HBM per device.

v0:
```python
import jax
import jax.numpy as jnp
from jax import lax
from jax.sharding import PartitionSpec as P


def tile_products(
    running, tile_block, slot_rows, slot_cols, source, first_slot, last_slot, forward
):
    slot_count = tile_block.shape[0]
    group_size = min(32, slot_count)

    def one_group(group_index, partial_value):
        group_begin = first_slot + group_index * group_size
        slot_start = jnp.minimum(group_begin, slot_count - group_size)
        slot_ids = slot_start + jnp.arange(group_size, dtype=jnp.int32)
        keep_mask = (
            (slot_ids >= group_begin)
            & (slot_ids < last_slot)
            & (slot_ids < group_begin + group_size)
        )
        tiles_now = (
            lax.dynamic_slice_in_dim(tile_block, slot_start, group_size, 0)
            * keep_mask.astype(tile_block.dtype)[:, None, None]
        )
        rows_now = lax.dynamic_slice_in_dim(slot_rows, slot_start, group_size, 0)
        cols_now = lax.dynamic_slice_in_dim(slot_cols, slot_start, group_size, 0)
        if forward:
            picked = source[cols_now]
            products = jnp.einsum(
                "gab,gbf->gaf", tiles_now, picked, preferred_element_type=jnp.float32
            )
            return partial_value.at[rows_now].add(products)
        picked = source[rows_now]
        products = jnp.einsum("gab,gaf->gbf", tiles_now, picked, preferred_element_type=jnp.float32)
        return partial_value.at[cols_now].add(products)

    group_total = (jnp.maximum(last_slot - first_slot, 0) + group_size - 1) // group_size
    return lax.fori_loop(0, group_total, one_group, running)


def local(feats, weight, cotangent, tile_values, tile_rows, tile_cols, tile_count):
    feature_width = feats.shape[2]
    local_rows = feats.shape[1]
    tile_block = tile_values[0, 0]
    slot_rows = tile_rows[0, 0]
    slot_cols = tile_cols[0, 0]
    tile_total = tile_count[0, 0]
    row_tiles = local_rows * lax.axis_size("col") // 128
    col_tiles = local_rows * lax.axis_size("row") // 128
    node_total = local_rows * lax.axis_size("row") * lax.axis_size("col")
    panel_rows = lax.all_gather(feats[0], "row", axis=0, tiled=True)
    panel_tiles = panel_rows.reshape(col_tiles, 128, feature_width)
    forward_part = jnp.zeros((row_tiles, 128, feature_width), jnp.float32)
    backward_part = jnp.zeros((col_tiles, 128, feature_width), jnp.float32)
    forward_part = tile_products(
        forward_part, tile_block, slot_rows, slot_cols, panel_tiles, 0, tile_total, True
    )
    summed = lax.psum_scatter(
        forward_part.reshape(row_tiles * 128, feature_width).astype(jnp.bfloat16),
        "col",
        scatter_dimension=0,
        tiled=True,
    )
    hidden = jnp.dot(summed, weight, preferred_element_type=jnp.float32)
    sigmoid_part = jax.nn.sigmoid(hidden)
    layer_out = (hidden * sigmoid_part).astype(jnp.bfloat16)
    hidden_grad = (
        cotangent[0].astype(jnp.float32) * sigmoid_part * (1.0 + hidden * (1.0 - sigmoid_part))
    ).astype(jnp.bfloat16)
    grad_rows = lax.dot_general(
        hidden_grad, weight, (((1,), (1,)), ((), ())), preferred_element_type=jnp.float32
    ).astype(jnp.bfloat16)
    weight_term = lax.dot_general(
        summed, hidden_grad, (((0,), (0,)), ((), ())), preferred_element_type=jnp.float32
    ) * node_total ** (-0.5)
    weight_grad = lax.psum(weight_term, ("row", "col"))
    gathered_grads = lax.all_gather(grad_rows, "col", axis=0, tiled=True).reshape(
        row_tiles, 128, feature_width
    )
    backward_part = tile_products(
        backward_part, tile_block, slot_rows, slot_cols, gathered_grads, 0, tile_total, False
    )
    feat_grad = lax.psum_scatter(
        backward_part.reshape(col_tiles * 128, feature_width).astype(jnp.bfloat16),
        "row",
        scatter_dimension=0,
        tiled=True,
    )
    return (layer_out[None], feat_grad[None], weight_grad)


def solution(mesh):
    in_specs = (
        P("col", "row", None),
        P(),
        P("row", "col", None),
        P("row", "col", None, None, None),
        P("row", "col", None),
        P("row", "col", None),
        P("row", "col"),
    )
    out_specs = (P("row", "col", None), P("col", "row", None), P())
    return jax.shard_map(local, mesh=mesh, in_specs=in_specs, out_specs=out_specs, check_vma=False)
```

profile of v0, /device:TPU:1, one launch (start us, length us, event | category | flops | bytes accessed | tf_op | source)
XLA Modules:
  0.0 700.4 jit_solution(4840851839593031856)
XLA Ops:
  7.2 0.0 copy-start
  7.2 0.0 all-gather.6.cloned.1.call-start
  7.2 0.7 all-gather.6.cloned.1.call-update
  7.9 0.0 reduce-scatter.3.cloned.1.call-start
  8.6 55.8 %all-gather.6.cloned.1.call-done = bf16[1,1024,512]{2,1,0:T(8,128)(2,1)} async-done(((bf16[1,128,512]{2,1,0:T(8,128)(2,1)}), bf16[1,1024,512]{2,1,0:T(8,128)(2,1)}) %all-gather.6.cloned.1.call-update) | async-done | bytes 1048592 | tf_op jit(solution)/shard_map/all_gather | solution.py:52
  64.5 4.3 broadcast_in_dim.26
  68.8 58.2 %while.20 = (s32[]{:T(128)}, f32[32,128,512]{2,1,0:T(8,128)}, s32[]{:T(128)}, s32[96]{0:T(128)S(1)}, bf16[96,128,128]{2,1,0:T(8,128)(2,1)}, /*index=5*/s32[]{:T(...) while((s32[]{:T(128)}, f32[32,128,512]{2,1,0:T(8,128)}, ...), condition=%wide.region_2.3_spmd, body=%wide.region_0.2_spmd.sunk | while | flops 539493824 | bytes 47191256 | solution.py:39
  68.8 0.1 compare_select_fusion.6
  68.9 2.8 gather_fusion
  71.7 0.7 and_convert_fusion.4
  72.3 7.0 %fusion.30 = f32[32,128,512]{2,1,0:T(8,128)} fusion(bf16[32,128,512]{2,1,0:T(8,128)(2,1)} %gather_fusion, bf16[96,128,128]{2,1,0:T(8,128)(2,1)} %get-tuple-element.273, s32[]{:T(128)S(6)} %select_n.38, bf16[32]{0:T(256)(128)(2,1)S(1)} %and_convert_fusion.4), kind=kOutput, calls=%fused_computation.4.clone.1 | convolution fusion | flops 537395200 | bytes 13631556 | tf_op jit(solution)/shard_map/while/body/gab,gbf->gaf/dot_general | solution.py:30
  79.4 18.4 %scatter_fusion = f32[32,128,512]{2,1,0:T(8,128)} fusion(f32[32,128,512]{2,1,0:T(8,128)} %get-tuple-element.257, s32[32]{0:T(128)S(1)} %get-tuple-element.231, f32[32,128,512]{2,1,0:T(8,128)} %fusion.30), kind=kCustom, calls=%fused_computation.2.clone.1 | custom fusion | flops 2097152 | bytes 25165952 | tf_op jit(solution)/shard_map/while/body/scatter-add | solution.py:33
  97.8 0.1 compare_select_fusion.6
  97.8 2.8 gather_fusion
  100.6 0.7 and_convert_fusion.4
  101.3 7.0 %fusion.30 = f32[32,128,512]{2,1,0:T(8,128)} fusion(bf16[32,128,512]{2,1,0:T(8,128)(2,1)} %gather_fusion, bf16[96,128,128]{2,1,0:T(8,128)(2,1)} %get-tuple-element.273, s32[]{:T(128)S(6)} %select_n.38, bf16[32]{0:T(256)(128)(2,1)S(1)} %and_convert_fusion.4), kind=kOutput, calls=%fused_computation.4.clone.1 | convolution fusion | flops 537395200 | bytes 13631556 | tf_op jit(solution)/shard_map/while/body/gab,gbf->gaf/dot_general | solution.py:30
  108.3 18.6 %scatter_fusion = f32[32,128,512]{2,1,0:T(8,128)} fusion(f32[32,128,512]{2,1,0:T(8,128)} %get-tuple-element.257, s32[32]{0:T(128)S(1)} %get-tuple-element.231, f32[32,128,512]{2,1,0:T(8,128)} %fusion.30), kind=kCustom, calls=%fused_computation.2.clone.1 | custom fusion | flops 2097152 | bytes 25165952 | tf_op jit(solution)/shard_map/while/body/scatter-add | solution.py:33
  126.9 6.0 convert_element_type.41
  132.9 0.0 reduce-scatter.3.cloned.1.call-update
  132.9 0.0 all-gather.4.cloned.1.call-start
  133.0 148.7 %reduce-scatter.3.cloned.1.call-done = bf16[128,512]{1,0:T(8,128)(2,1)} async-done(((bf16[4096,512]{1,0:T(8,128)(2,1)}), bf16[128,512]{1,0:T(8,128)(2,1)}) %reduce-scatter.3.cloned.1.call-update) | async-done | bytes 131088 | tf_op jit(solution)/shard_map/reduce_scatter | solution.py:59
  281.6 1.1 fusion.15
  282.8 1.0 convolution_convert_fusion
  283.8 0.0 all-gather.4.cloned.1.call-update
  283.8 0.0 all-reduce.2.cloned.1.call-start
  283.8 4.7 copy.10
  288.5 1.3 convolution_multiply_fusion
  289.8 0.0 all-reduce.2.cloned.1.call-update
  289.9 0.0 reduce-scatter.5.cloned.1.call-start
  289.9 62.8 %all-gather.4.cloned.1.call-done = bf16[4096,512]{1,0:T(8,128)(2,1)} async-done(((bf16[128,512]{1,0:T(8,128)(2,1)}), bf16[4096,512]{1,0:T(8,128)(2,1)}) %all-gather.4.cloned.1.call-update) | async-done | bytes 4194320 | tf_op jit(solution)/shard_map/all_gather | solution.py:78
  352.7 0.2 broadcast_in_dim.28
  353.0 49.1 %while.21 = (s32[]{:T(128)}, f32[8,128,512]{2,1,0:T(8,128)S(1)}, s32[]{:T(128)}, s32[96]{0:T(128)S(1)}, bf16[96,128,128]{1,2,0:T(8,128)(2,1)}, /*index=5*/s32[]{...) while((s32[]{:T(128)}, f32[8,128,512]{2,1,0:T(8,128)S(1)}, ...), condition=%wide.region_6.7_spmd, body=%wide.region_4.6_spmd.sunk | while | flops 539493824 | bytes 47191256 | solution.py:39
  353.0 0.1 compare_select_fusion.7
  353.1 4.9 gather_fusion.1
  358.1 0.7 and_convert_fusion.5
  358.7 7.0 %fusion.33 = f32[32,128,512]{2,1,0:T(8,128)} fusion(bf16[32,128,512]{2,1,0:T(8,128)(2,1)} %gather_fusion.1, bf16[96,128,128]{1,2,0:T(8,128)(2,1)} %get-tuple-element.312, s32[]{:T(128)S(6)} %select_n.40, bf16[32]{0:T(256)(128)(2,1)S(1)} %and_convert_fusion.5), kind=kOutput, calls=%fused_computation.13.clone.1 | convolution fusion | flops 537395200 | bytes 13631556 | tf_op jit(solution)/shard_map/while/body/gab,gaf->gbf/dot_general | solution.py:35
  365.7 11.7 %scatter_fusion.1 = f32[8,128,512]{2,1,0:T(8,128)S(1)} fusion(f32[8,128,512]{2,1,0:T(8,128)S(1)} %get-tuple-element.296, s32[32]{0:T(128)S(1)} %get-tuple-element.241, f32[32,128,512]{2,1,0:T(8,128)} %fusion.33), kind=kCustom, calls=%fused_computation.3.clone.1 | custom fusion | flops 2097152 | bytes 25165952 | tf_op jit(solution)/shard_map/while/body/scatter-add | solution.py:36
  377.5 0.1 compare_select_fusion.7
  377.6 5.0 gather_fusion.1
  382.6 0.7 and_convert_fusion.5
  383.2 7.1 %fusion.33 = f32[32,128,512]{2,1,0:T(8,128)} fusion(bf16[32,128,512]{2,1,0:T(8,128)(2,1)} %gather_fusion.1, bf16[96,128,128]{1,2,0:T(8,128)(2,1)} %get-tuple-element.312, s32[]{:T(128)S(6)} %select_n.40, bf16[32]{0:T(256)(128)(2,1)S(1)} %and_convert_fusion.5), kind=kOutput, calls=%fused_computation.13.clone.1 | convolution fusion | flops 537395200 | bytes 13631556 | tf_op jit(solution)/shard_map/while/body/gab,gaf->gbf/dot_general | solution.py:35
  390.3 11.8 %scatter_fusion.1 = f32[8,128,512]{2,1,0:T(8,128)S(1)} fusion(f32[8,128,512]{2,1,0:T(8,128)S(1)} %get-tuple-element.296, s32[32]{0:T(128)S(1)} %get-tuple-element.241, f32[32,128,512]{2,1,0:T(8,128)} %fusion.33), kind=kCustom, calls=%fused_computation.3.clone.1 | custom fusion | flops 2097152 | bytes 25165952 | tf_op jit(solution)/shard_map/while/body/scatter-add | solution.py:36
  402.1 1.1 convert_element_type.48
  403.2 0.0 reduce-scatter.5.cloned.1.call-update
  403.2 0.7 fusion.12
  404.0 207.8 %all-reduce.2.cloned.1.call-done = f32[512,512]{1,0:T(8,128)} async-done(((f32[512,512]{1,0:T(8,128)}), f32[512,512]{1,0:T(8,128)}) %all-reduce.2.cloned.1.call-update) | async-done | bytes 1048592 | tf_op jit(solution)/shard_map/psum | solution.py:77
  611.7 79.9 %reduce-scatter.5.cloned.1.call-done = bf16[128,512]{1,0:T(8,128)(2,1)} async-done(((bf16[1024,512]{1,0:T(8,128)(2,1)}), bf16[128,512]{1,0:T(8,128)(2,1)}) %reduce-scatter.5.cloned.1.call-update) | async-done | bytes 131088 | tf_op jit(solution)/shard_map/reduce_scatter | solution.py:84
  691.6 2.3 copy.29
  (15 shorter events, 0.0 us)
Async XLA Ops:
  7.2 274.5 %copy-start = (bf16[512,512]{1,0:T(8,128)(2,1)S(1)}, bf16[512,512]{1,0:T(8,128)(2,1)}, u32[]{:S(2)}) copy-start(bf16[512,512]{1,0:T(8,128)(2,1)} %param.12) | copy-start | bytes 1572868
  7.2 57.3 %all-gather.6.cloned.1.call-start = ((), (), s32[]{:S(2)}) async-start(), calls=%async_computation.6 | async-start | bytes 1179648 | tf_op jit(solution)/shard_map/all_gather | solution.py:52
  7.9 273.7 %reduce-scatter.3.cloned.1.call-start = ((), (), s32[]{:S(2)}) async-start(), calls=%async_computation.2 | async-start | bytes 4325376 | tf_op jit(solution)/shard_map/reduce_scatter | solution.py:59
  64.5 4.3 copy-start.1
  64.5 4.3 copy-start.3
  64.5 4.3 copy-start.4
  132.9 149.9 %copy-start.5 = (bf16[1,128,512]{2,1,0:T(8,128)(2,1)S(1)}, bf16[1,128,512]{2,1,0:T(8,128)(2,1)}, u32[]{:S(2)}) copy-start(bf16[1,128,512]{2,1,0:T(8,128)(2,1)} %param.13) | copy-start | bytes 393220
  132.9 219.8 %all-gather.4.cloned.1.call-start = ((), (), s32[]{:S(2)}) async-start(), calls=%async_computation.3 | async-start | bytes 4325376 | tf_op jit(solution)/shard_map/all_gather | solution.py:78
  282.8 5.7 copy-start.2
  283.8 327.9 %all-reduce.2.cloned.1.call-start = ((), (), s32[]{:S(2)}) async-start(), calls=%async_computation.5 | async-start | bytes 2097152 | tf_op jit(solution)/shard_map/psum | solution.py:77
  289.9 401.7 %reduce-scatter.5.cloned.1.call-start = ((), (), s32[]{:S(2)}) async-start(), calls=%async_computation.4 | async-start | bytes 1179648 | tf_op jit(solution)/shard_map/reduce_scatter | solution.py:84
Sparse Core Ops, SparseCore 0:
  10.7 53.7 all-gather.5
  133.0 148.5 reduce-scatter.2
  284.1 68.6 all-gather.3
  358.0 253.6 all-reduce.1
  616.5 75.0 reduce-scatter.4
where the time goes:
time: 702 us; the launch traced here: 700 us
  waiting for transfers between devices  556 us (79%)
  other arithmetic  71.3 us (10%)
  matrix products  31.6 us (5%)
  local copies, waits for them, and re-layouts  26.9 us (4%)
  between operations  14.5 us (2%)
    psum x1, waiting for transfers between devices, local(): weight_grad = lax.psum(weight_term, ('row', 'col'))  208 us
    reduce_scatter x1, waiting for transfers between devices, local(): lax.psum_scatter(forward_part.reshape(row_tiles * 128, feature_width).ast...  149 us
    reduce_scatter x1, waiting for transfers between devices, local(): lax.psum_scatter(backward_part.reshape(col_tiles * 128, feature_width).as...  79.9 us
    all_gather x1, waiting for transfers between devices, local(): lax.all_gather(grad_rows, 'col', axis=0, tiled=True)  62.8 us
    all_gather x1, waiting for transfers between devices, local(): panel_rows = lax.all_gather(feats[0], 'row', axis=0, tiled=True)  55.8 us
    scatter-add x2, other arithmetic, one_group(): return partial_value.at[rows_now].add(products)  37 us
    scatter-add x2, other arithmetic, one_group(): return partial_value.at[cols_now].add(products)  23.5 us
    dot_general x2, matrix products, one_group(): jnp.einsum('gab,gaf->gbf', tiles_now, picked, preferred_element_type=jnp....  14.1 us
  transfers between devices with their start and end apart: 5, of which 5 were waited for; matrix products, arithmetic and copies ran while one was open for 8% of the time, Pallas kernels for 0%

commit v1 on v0

v1 whole, which is shorter than its diff:
```python
import functools

import jax
import jax.numpy as jnp
from jax import lax
from jax.experimental import pallas as pl
from jax.experimental.pallas import tpu as pltpu
from jax.sharding import PartitionSpec as P

BF = jnp.bfloat16
F32 = jnp.float32
X_HI, X_LO, CORE = 2, 2, 2


def layer_kernel(
    n_row, n_col, tab, feats, weight, cot, tiles_hbm, layer_out, feat_grad, weight_grad,
    tiles, dense, panel, part, core_in, rp, rm, own_sum, x_in, gath, acc, back, yp, ym, xb_in,
    w_term, w_core, wy_p, wy_m, w_y, wx_p, wx_m, w_x, w_z,
    tile_sem, send_sems, recv_sems, core_send, core_recv,
):
    Y, Z = n_row // X_HI, n_col // (X_LO * CORE)
    X = X_HI * X_LO
    HZ = Z // 2
    slots = tiles_hbm.shape[0]
    row_tiles, col_tiles = tab.shape
    chunk = row_tiles * 128 // Z
    width = feats.shape[1]

    r, c = lax.axis_index("row"), lax.axis_index("col")
    xh, y = r // Y, r % Y
    z, xl, k = c // (X_LO * CORE), (c // CORE) % X_LO, c % CORE
    x = xh * X_LO + xl

    def device(x_at, y_at, z_at, k_at):
        return ((x_at // X_LO) * Y + y_at, z_at * (X_LO * CORE) + (x_at % X_LO) * CORE + k_at)

    core_dev = device(x, y, z, 1 - k)
    x_plus, x_minus = device((x + 1) % X, y, z, k), device((x + X - 1) % X, y, z, k)
    x_far = device((x + 2) % X, y, z, k)
    x_near = device(xh * X_LO + 1 - xl, y, z, k)
    y_plus, y_minus = device(x, (y + 1) % Y, z, k), device(x, (y + Y - 1) % Y, z, k)
    z_plus, z_minus = device(x, y, (z + 1) % Z, k), device(x, y, (z + Z - 1) % Z, k)

    pending = []
    counters = {"send": 0, "recv": 0}

    def fresh():
        counters["recv"] += 1
        return counters["recv"] - 1

    def remote(src, dst, sem_out, sem_in, dev):
        return pltpu.make_async_remote_copy(
            src_ref=src, dst_ref=dst, send_sem=sem_out, recv_sem=sem_in,
            device_id=dev, device_id_type=pl.DeviceIdType.MESH,
        )

    def send(src, dst, sem, dev):
        copy = remote(src, dst, send_sems.at[counters["send"]], recv_sems.at[sem], dev)
        counters["send"] += 1
        copy.start()
        pending.append(copy)

    def arrived(view, sem):
        remote(view, view, send_sems.at[0], recv_sems.at[sem], core_dev).wait_recv()

    def add_into(dst, other):
        dst[...] = (dst[...].astype(F32) + other[...].astype(F32)).astype(dst.dtype)

    def ring_gather(pos, n, view, plus, minus, ready=None, on_block=None):
        half = n // 2
        sems = {(s, d, o): fresh() for s in (1, -1) for d in range(1, half + 1) for o in (0, 1)}

        def goes(s, d, o):
            return d < half or (d == half and o == (0 if s == 1 else 1))

        for o in (0, 1):
            if ready is not None:
                ready(o)
            for s in (1, -1):
                if goes(s, 1, o):
                    send(view(pos, o), view(pos, o), sems[s, 1, o], plus if s == 1 else minus)
        for d in range(1, half + 1):
            yield
            for o in (0, 1):
                for s in (1, -1):
                    if not goes(s, d, o):
                        continue
                    at = (pos - s * d + n) % n
                    arrived(view(at, o), sems[s, d, o])
                    if goes(s, d + 1, o):
                        send(view(at, o), view(at, o), sems[s, d + 1, o], plus if s == 1 else minus)
                    if on_block is not None:
                        on_block(at, o, s, d)

    def ring_sum(pos, n, view, bufs_p, bufs_m, plus, minus, before=None):
        half = n // 2
        bufs, dev = {1: bufs_p, -1: bufs_m}, {1: plus, -1: minus}
        sems = {(s, d, o): fresh() for s in (1, -1) for d in range(half) for o in (0, 1)}
        first = {(1, 0): half, (1, 1): half - 1, (-1, 1): half, (-1, 0): half - 1}
        for o in (0, 1):
            for s in (1, -1):
                d = first[s, o]
                if d > 0 and d == half:
                    send(view((pos + s * d + n) % n, o), bufs[s].at[d - 1, o], sems[s, d - 1, o], dev[s])
        for o in (1, 0):
            for s in (1, -1):
                d = first[s, o]
                if d > 0 and d < half:
                    send(view((pos + s * d + n) % n, o), bufs[s].at[d - 1, o], sems[s, d - 1, o], dev[s])
        for d in range(half - 1, 0, -1):
            yield
            if before is not None:
                before(d)
            for o in (1, 0):
                for s in (1, -1):
                    if d >= first[s, o]:
                        continue
                    buf = bufs[s].at[d, o]
                    arrived(buf, sems[s, d, o])
                    add_into(buf, view((pos + s * d + n) % n, o))
                    send(buf, bufs[s].at[d - 1, o], sems[s, d - 1, o], dev[s])
        yield
        if before is not None:
            before(0)

        def total(o):
            value = view(pos, o)[...].astype(F32)
            for s in (1, -1):
                if first[s, o] > 0:
                    arrived(bufs[s].at[0, o], sems[s, 0, o])
                    value = value + bufs[s][0, o].astype(F32)
            return value

        return total

    tile_copy = pltpu.make_async_copy(tiles_hbm, tiles.at[pl.ds(0, slots)], tile_sem)
    tile_copy.start()
    barrier = pltpu.get_barrier_semaphore()
    peers = (core_dev, x_plus, x_minus, x_far, y_plus, y_minus, z_plus, z_minus)
    for dev in peers:
        pl.semaphore_signal(barrier, inc=1, device_id=dev, device_id_type=pl.DeviceIdType.MESH)
    tiles[slots] = jnp.zeros(tiles.shape[1:], tiles.dtype)
    pl.semaphore_wait(barrier, len(peers))

    def panel_at(at, o):
        return panel.at[(xh if o == 0 else 1 - xh) * Y + at]

    panel[xh * Y + y] = feats[...]
    far_sem = fresh()
    send(feats, panel_at(y, 0), far_sem, x_far)

    def densify():
        tile_copy.wait()

        def one_row(i, carry):
            for j in range(col_tiles):
                dense[pl.ds(pl.multiple_of(i * 128, 128), 128), j * 128 : (j + 1) * 128] = tiles[tab[i, j]]
            return carry

        lax.fori_loop(0, row_tiles, one_row, 0)

    def panel_ready(o):
        if o == 1:
            densify()
            arrived(panel_at(y, 1), far_sem)

    for _ in ring_gather(y, Y, panel_at, y_plus, y_minus, ready=panel_ready):
        pass

    def forward_chunk(t, carry):
        off = HZ + (1 - 2 * (t % 2)) * ((t + 1) // 2)
        at = (z + off) % Z
        product = jnp.dot(
            dense[pl.ds(pl.multiple_of(at * chunk, chunk), chunk), :],
            panel[...].reshape(col_tiles * 128, width),
            preferred_element_type=F32,
        )
        part[at] = product.astype(BF).reshape(X_LO, CORE, 128, width)
        remote(
            part.at[at, :, 1 - k], core_in.at[at], core_send.at[t], core_recv.at[t], core_dev
        ).start()
        return carry

    def core_total(t):
        off = HZ + (1 - 2 * (t % 2)) * ((t + 1) // 2)
        at = (z + off) % Z
        remote(
            part.at[at, :, 1 - k], core_in.at[at], core_send.at[t], core_recv.at[t], core_dev
        ).wait()
        for o in range(X_LO):
            add_into(core_in.at[at, o], part.at[at, o, k])

    def sum_at(at, o):
        return core_in.at[at, xl if o == 0 else 1 - xl]

    lax.fori_loop(0, 3, forward_chunk, 0)
    for t in range(3):
        core_total(t)

    done = [3]

    def before(d):
        if d == HZ - 1:
            lax.fori_loop(3, Z, forward_chunk, 0)
        while done[0] < Z and d <= HZ - 2 and done[0] <= 2 * (HZ - d):
            core_total(done[0])
            done[0] += 1

    steps = ring_sum(z, Z, sum_at, rp, rm, z_plus, z_minus, before=before)
    while True:
        try:
            next(steps)
        except StopIteration as stop:
            total = stop.value
            break
    x_sem = fresh()
    own_sum[...] = total(1).astype(BF)
    send(own_sum, x_in, x_sem, x_near)
    mine = total(0)
    arrived(x_in, x_sem)
    summed = (mine + x_in[...].astype(F32)).astype(BF)

    hidden = jnp.dot(summed, weight[...], preferred_element_type=F32)
    gate = jax.nn.sigmoid(hidden)
    hidden_grad = (cot[...].astype(F32) * gate * (1.0 + hidden * (1.0 - gate))).astype(BF)
    grad_rows = lax.dot_general(
        hidden_grad, weight[...], (((1,), (1,)), ((), ())), preferred_element_type=F32
    ).astype(BF)
    gath[z, xl, k] = grad_rows

    near_sem = fresh()

    def gath_at(at, o):
        return gath.at[at, xl if o == 0 else 1 - xl, k]

    def gath_other(at, o):
        return gath.at[at, xl if o == 0 else 1 - xl, 1 - k]

    pair_sems = {}

    def to_core(at, o, s, d):
        key = (o, s, d)
        pair_sems[key] = fresh()
        send(gath_at(at, o), gath_at(at, o), pair_sems[key], core_dev)

    send(gath_at(z, 0), gath_at(z, 0), near_sem, x_near)

    def gath_ready(o):
        if o == 1:
            to_core(z, 0, 1, 0)
            layer_out[...] = (hidden * gate).astype(BF)
            w_term[...] = (
                lax.dot_general(summed, hidden_grad, (((0,), (0,)), ((), ())), preferred_element_type=F32)
                * (n_row * n_col * 128) ** (-0.5)
            ).reshape(w_term.shape)
            arrived(gath_at(z, 1), near_sem)

    def backward_chunk(at):
        product = lax.dot_general(
            dense[pl.ds(pl.multiple_of(at * chunk, chunk), chunk), :],
            gath[at].reshape(chunk, width),
            (((0,), (0,)), ((), ())),
            preferred_element_type=F32,
        )
        return product

    def accumulate(keys, at, start=False):
        for o, s, d in keys:
            arrived(gath_other(at, o), pair_sems[o, s, d])
        if start:
            acc[...] = backward_chunk(at)
        else:
            acc[...] += backward_chunk(at)

    def weight_steps():
        sem = fresh()
        send(w_term.at[1 - k], w_core, sem, core_dev)
        yield
        arrived(w_core, sem)
        add_into(w_core, w_term.at[k])
        total = yield from ring_sum(
            y, Y, lambda at, o: w_core.at[at, o], wy_p, wy_m, y_plus, y_minus
        )
        for o in (0, 1):
            w_y[o] = total(o).reshape(w_y.shape[1:])
        total = yield from ring_sum(
            x, X, lambda at, o: w_y.at[at // 2, at % 2, o], wx_p, wx_m, x_plus, x_minus
        )
        for o in (0, 1):
            w_z[z, o] = total(o)
        yield from ring_gather(z, Z, lambda at, o: w_z.at[at, o], z_plus, z_minus)
        full = w_z[0]
        for at in range(1, Z):
            full = full + w_z[at]
        w_x[k, y, x] = full
        yield from ring_gather(x, X, lambda at, o: w_x.at[k, y, at, o], x_plus, x_minus)
        yield from ring_gather(
            y, Y, lambda at, o: w_x.at[k, at, pl.ds(o * (X // 2), X // 2)], y_plus, y_minus
        )
        sem = fresh()
        send(w_x.at[k], w_x.at[k], sem, core_dev)
        yield
        arrived(w_x.at[1 - k], sem)

    weight_run = weight_steps()

    def weight_step(count):
        for _ in range(count):
            next(weight_run, None)

    gather_run = ring_gather(z, Z, gath_at, z_plus, z_minus, ready=gath_ready, on_block=to_core)
    next(gather_run)
    to_core(z, 1, 1, 0)
    weight_step(1)
    accumulate([(0, 1, 0), (1, 1, 0)], z, start=True)
    weight_step(1)
    for d in range(1, HZ + 1):
        next(gather_run, None)
        weight_step(2)
        if d < HZ:
            for s in (1, -1):
                accumulate([(0, s, d), (1, s, d)], (z - s * d + Z) % Z)
        else:
            accumulate([(0, 1, d), (1, -1, d)], (z + HZ) % Z)
        weight_step(2)

    back[...] = acc[...].astype(BF).reshape(back.shape)

    def back_at(at, o):
        return back.at[xh if o == 0 else 1 - xh, at]

    steps = ring_sum(y, Y, back_at, yp, ym, y_plus, y_minus)
    while True:
        try:
            next(steps)
            weight_step(1)
        except StopIteration as stop:
            total = stop.value
            break
    far_back = fresh()
    own_sum2 = yp.at[1, 1]
    own_sum2[...] = total(1).astype(BF)
    send(own_sum2, xb_in, far_back, x_far)
    mine = total(0)
    for _ in weight_run:
        pass
    weight_grad[...] = w_x[...].reshape(weight_grad.shape)
    arrived(xb_in, far_back)
    feat_grad[...] = (mine + xb_in[...].astype(F32)).astype(BF)
    for copy in pending:
        copy.wait_send()
    assert counters["send"] <= send_sems.shape[0] and counters["recv"] <= recv_sems.shape[0]


def local(n_row, n_col, feats, weight, cotangent, tile_values, tile_rows, tile_cols, tile_count):
    rows_here, width = feats.shape[1:]
    slots = tile_values.shape[2]
    Y, Z, X = n_row // X_HI, n_col // (X_LO * CORE), X_HI * X_LO
    row_tiles, col_tiles = n_col, n_row
    ids = tile_rows[0, 0] * col_tiles + tile_cols[0, 0]
    slot_ids = jnp.arange(slots, dtype=jnp.int32)
    ids = jnp.where(slot_ids < tile_count[0, 0], ids, -1)
    places = jnp.arange(row_tiles * col_tiles, dtype=jnp.int32)
    hit = ids[None, :] == places[:, None]
    tab = jnp.min(jnp.where(hit, slot_ids[None, :], slots), axis=1).reshape(row_tiles, col_tiles)

    block = (128, width)
    w_rows = width // (CORE * Y * X)
    scratch = [
        pltpu.VMEM((slots + 1, 128, 128), BF),
        pltpu.VMEM((row_tiles * 128, col_tiles * 128), BF),
        pltpu.VMEM((n_row,) + block, BF),
        pltpu.VMEM((Z, X_LO, CORE) + block, BF),
        pltpu.VMEM((Z, X_LO) + block, BF),
        pltpu.VMEM((Z // 2, 2) + block, BF),
        pltpu.VMEM((Z // 2, 2) + block, BF),
        pltpu.VMEM(block, BF),
        pltpu.VMEM(block, BF),
        pltpu.VMEM((Z, X_LO, CORE) + block, BF),
        pltpu.VMEM((col_tiles * 128, width), F32),
        pltpu.VMEM((X_HI, Y) + block, BF),
        pltpu.VMEM((Y // 2, 2) + block, BF),
        pltpu.VMEM((Y // 2, 2) + block, BF),
        pltpu.VMEM(block, BF),
        pltpu.VMEM((CORE, Y, 2, X * w_rows // 2, width), F32),
        pltpu.VMEM((Y, 2, X * w_rows // 2, width), F32),
        pltpu.VMEM((Y // 2, 2, X * w_rows // 2, width), F32),
        pltpu.VMEM((Y // 2, 2, X * w_rows // 2, width), F32),
        pltpu.VMEM((2, X // 2, 2, w_rows // 2, width), F32),
        pltpu.VMEM((X // 2, 2, w_rows // 2, width), F32),
        pltpu.VMEM((X // 2, 2, w_rows // 2, width), F32),
        pltpu.VMEM((CORE, Y, X, 2, w_rows // 2, width), F32),
        pltpu.VMEM((Z, 2, w_rows // 2, width), F32),
        pltpu.SemaphoreType.DMA,
        pltpu.SemaphoreType.DMA((140,)),
        pltpu.SemaphoreType.DMA((170,)),
        pltpu.SemaphoreType.DMA((Z,)),
        pltpu.SemaphoreType.DMA((Z,)),
    ]
    vmem = pl.BlockSpec(memory_space=pltpu.VMEM)
    layer_out, feat_grad, weight_grad = pl.pallas_call(
        functools.partial(layer_kernel, n_row, n_col),
        out_shape=(
            jax.ShapeDtypeStruct(block, BF),
            jax.ShapeDtypeStruct(block, BF),
            jax.ShapeDtypeStruct((width, width), F32),
        ),
        in_specs=[
            pl.BlockSpec(memory_space=pltpu.SMEM), vmem, vmem, vmem,
            pl.BlockSpec(memory_space=pl.ANY),
        ],
        out_specs=(vmem, vmem, vmem),
        scratch_shapes=scratch,
        compiler_params=pltpu.CompilerParams(
            collective_id=0, has_side_effects=True, vmem_limit_bytes=60 * 1024 * 1024
        ),
    )(tab, feats[0], weight, cotangent[0], tile_values[0, 0])
    return layer_out[None], feat_grad[None], weight_grad


def solution(mesh):
    in_specs = (
        P("col", "row", None),
        P(),
        P("row", "col", None),
        P("row", "col", None, None, None),
        P("row", "col", None),
        P("row", "col", None),
        P("row", "col"),
    )
    out_specs = (P("row", "col", None), P("col", "row", None), P())
    return jax.shard_map(
        functools.partial(local, mesh.shape["row"], mesh.shape["col"]),
        mesh=mesh, in_specs=in_specs, out_specs=out_specs, check_vma=False,
    )
```

time: 702 us -> 132 us (0.19)
  waiting for transfers between devices: 556 us -> 0 us
  Pallas kernels: 0 us -> 124 us
  other arithmetic: 71.3 us -> 0.77 us
  matrix products: 31.6 us -> 0 us
  local copies, waits for them, and re-layouts: 26.9 us -> 6.1 us
  between operations: 14.5 us -> 1.29 us
    reduce_scatter x2 -> x0, waiting for transfers between devices: 229 us -> none  [the longest x1 149 us: local(): lax.psum_scatter(forward_part.reshape(row_tiles * 128, feature_width).ast...]
    psum x1 -> x0, waiting for transfers between devices: 208 us -> none  [local(): weight_grad = lax.psum(weight_term, ('row', 'col'))]
    pallas_call x0 -> x1, Pallas kernels: none -> 124 us  [local(): pl.pallas_call(functools.partial(layer_kernel, n_row, n_col), out_shape=(...]
    all_gather x2 -> x0, waiting for transfers between devices: 119 us -> none  [the longest x1 62.8 us: local(): lax.all_gather(grad_rows, 'col', axis=0, tiled=True)]
    scatter-add x4 -> x0, other arithmetic: 60.6 us -> none  [the longest x2 37 us: one_group(): return partial_value.at[rows_now].add(products)]
    dot_general x7 -> x0, matrix products: 31.6 us -> none  [the longest x2 14.1 us: one_group(): jnp.einsum('gab,gaf->gbf', tiles_now, picked, preferred_element_type=jnp....]
    gather x4 -> x0, local copies, waits for them, and re-layouts: 15.4 us -> none  [the longest x2 9.89 us: one_group(): picked = source[rows_now]]
    convert_element_type x6 -> x0, other arithmetic: 9.66 us -> none  [the longest x1 5.96 us: local(): forward_part.reshape(row_tiles * 128, feature_width).astype(jnp.bfloat16)]
  transfers between devices with their start and end apart: 5 -> 0, of which waited for: 5 -> 0; matrix products, arithmetic and copies ran while one was open for 8% -> 0% of each run, Pallas kernels for 0% -> 0%
where the time goes in v1:
time: 132 us
  Pallas kernels  124 us (94%)
  local copies, waits for them, and re-layouts  6.1 us (5%)
    pallas_call x1, Pallas kernels, local(): pl.pallas_call(functools.partial(layer_kernel, n_row, n_col), out_shape=(...  124 us
    unnamed x3, local copies, waits for them, and re-layouts  5.4 us

profile of v1, /device:TPU:1, one launch (start us, length us, event | category | flops | bytes accessed | tf_op | source)
XLA Modules:
  0.0 131.8 jit_solution(12387874984648012791)
XLA Ops:
  1.3 0.7 compare_select_fusion
  2.0 0.1 select_reduce_fusion
  2.1 0.7 reshape.27.tab
  2.8 123.6 %shard_map.94 = (bf16[128,512]{1,0:T(8,128)(2,1)}, bf16[128,512]{1,0:T(8,128)(2,1)}, f32[512,512]{1,0:T(8,128)}) custom-call(s32[32,8]{1,0:T(8,128)} %reshape.27.tab, bf16[128,512]{1,0:T(8,128)(2,1)} %bitcast.10, bf16[512,512]{1,0:T(8,128)(2,1)} %weight.1, bf16[128,512]{1,0:T(8,128)(2,1)} %bitcast.11, bf16[96,128,128]{2,1,0:T(8,128)(2,1)} %bitcast.9), custom_call_target="tpu_custom_call" | custom-call | tf_op jit(solution)/shard_map/pallas_call | solution.py:401
  126.4 1.6 %copy.14 = bf16[1,128,512]{2,1,0:T(8,128)(2,1)} copy(bf16[1,128,512]{2,1,0:T(8,128)(2,1)} %bitcast.13) | data formatting | bytes 262144
  127.9 1.6 %copy.15 = bf16[1,128,512]{2,1,0:T(8,128)(2,1)} copy(bf16[1,128,512]{2,1,0:T(8,128)(2,1)} %bitcast.12) | data formatting | bytes 262144
  129.5 2.3 %copy.16 = f32[512,512]{1,0:T(8,128)} copy(f32[512,512]{1,0:T(8,128)} %get-tuple-element.14) | data formatting | bytes 2097152

commit v2 on v1

--- a/solution.py
+++ b/solution.py
@@ -13,18 +13,19 @@
 
 
 def layer_kernel(
-    n_row, n_col, tab, feats, weight, cot, tiles_hbm, layer_out, feat_grad, weight_grad,
-    tiles, dense, panel, part, core_in, rp, rm, own_sum, x_in, gath, acc, back, yp, ym, xb_in,
+    n_row, n_col, tab, feats_hbm, weight_hbm, cot_hbm, tiles_hbm, layer_hbm, feat_grad_hbm, weight_grad_hbm,
+    weight, cot, layer_out, feat_grad, tiles, dense, panel, part, core_in, rp, rm, own_sum, x_in, gath, acc, back, yp, ym, xb_in,
     w_term, w_core, wy_p, wy_m, w_y, wx_p, wx_m, w_x, w_z,
-    tile_sem, send_sems, recv_sems, core_send, core_recv,
+    tile_sem, local_sems, send_sems, recv_sems, core_send, core_recv,
 ):
     Y, Z = n_row // X_HI, n_col // (X_LO * CORE)
     X = X_HI * X_LO
     HZ = Z // 2
-    slots = tiles_hbm.shape[0]
-    row_tiles, col_tiles = tab.shape
+    slots = tiles_hbm.shape[2]
+    row_tiles, col_tiles = n_col, n_row
     chunk = row_tiles * 128 // Z
-    width = feats.shape[1]
+    width = feats_hbm.shape[2]
+    half_rows = 64
 
     r, c = lax.axis_index("row"), lax.axis_index("col")
     xh, y = r // Y, r % Y
@@ -133,28 +134,34 @@
 
         return total
 
-    tile_copy = pltpu.make_async_copy(tiles_hbm, tiles.at[pl.ds(0, slots)], tile_sem)
+    def panel_at(at, o):
+        return panel.at[(xh if o == 0 else 1 - xh) * Y + at]
+
+    feats_copy = pltpu.make_async_copy(feats_hbm.at[0], panel_at(y, 0), local_sems.at[0])
+    feats_copy.start()
+    weight_copy = pltpu.make_async_copy(weight_hbm, weight, local_sems.at[1])
+    cot_copy = pltpu.make_async_copy(cot_hbm.at[0], cot, local_sems.at[2])
+    tile_copy = pltpu.make_async_copy(tiles_hbm.at[0, 0], tiles.at[pl.ds(0, slots)], tile_sem)
     tile_copy.start()
     barrier = pltpu.get_barrier_semaphore()
     peers = (core_dev, x_plus, x_minus, x_far, y_plus, y_minus, z_plus, z_minus)
     for dev in peers:
         pl.semaphore_signal(barrier, inc=1, device_id=dev, device_id_type=pl.DeviceIdType.MESH)
+    weight_copy.start()
+    cot_copy.start()
     tiles[slots] = jnp.zeros(tiles.shape[1:], tiles.dtype)
+    feats_copy.wait()
     pl.semaphore_wait(barrier, len(peers))
 
-    def panel_at(at, o):
-        return panel.at[(xh if o == 0 else 1 - xh) * Y + at]
-
-    panel[xh * Y + y] = feats[...]
     far_sem = fresh()
-    send(feats, panel_at(y, 0), far_sem, x_far)
+    send(panel_at(y, 0), panel_at(y, 0), far_sem, x_far)
 
     def densify():
         tile_copy.wait()
 
         def one_row(i, carry):
             for j in range(col_tiles):
-                dense[pl.ds(pl.multiple_of(i * 128, 128), 128), j * 128 : (j + 1) * 128] = tiles[tab[i, j]]
+                dense[pl.ds(pl.multiple_of(i * 128, 128), 128), j * 128 : (j + 1) * 128] = tiles[tab[i * col_tiles + j]]
             return carry
 
         lax.fori_loop(0, row_tiles, one_row, 0)
@@ -220,6 +227,8 @@
     arrived(x_in, x_sem)
     summed = (mine + x_in[...].astype(F32)).astype(BF)
 
+    weight_copy.wait()
+    cot_copy.wait()
     hidden = jnp.dot(summed, weight[...], preferred_element_type=F32)
     gate = jax.nn.sigmoid(hidden)
     hidden_grad = (cot[...].astype(F32) * gate * (1.0 + hidden * (1.0 - gate))).astype(BF)
@@ -228,32 +237,49 @@
     ).astype(BF)
     gath[z, xl, k] = grad_rows
 
-    near_sem = fresh()
-
-    def gath_at(at, o):
-        return gath.at[at, xl if o == 0 else 1 - xl, k]
-
-    def gath_other(at, o):
-        return gath.at[at, xl if o == 0 else 1 - xl, 1 - k]
-
-    pair_sems = {}
-
-    def to_core(at, o, s, d):
-        key = (o, s, d)
-        pair_sems[key] = fresh()
-        send(gath_at(at, o), gath_at(at, o), pair_sems[key], core_dev)
-
-    send(gath_at(z, 0), gath_at(z, 0), near_sem, x_near)
+    def piece(at, p, core):
+        slot = xl if p == 0 else 1 - xl
+        if p == 0:
+            return gath.at[at, slot, core]
+        return gath.at[at, slot, core, pl.ds((p - 1) * half_rows, half_rows)]
+
+    def own_half(at, h):
+        return gath.at[at, xl, k, pl.ds(h * half_rows, half_rows)]
+
+    pair_sems, near_sems = {}, {}
+
+    def to_core(at, p, s, d):
+        pair_sems[p, s, d] = fresh()
+        send(piece(at, p, k), piece(at, p, k), pair_sems[p, s, d], core_dev)
+
+    def to_near(at, h, s, d):
+        near_sems[h, s, d] = fresh()
+        send(own_half(at, h), own_half(at, h), near_sems[h, s, d], x_near)
+
+    def from_near(at, h, s, d):
+        arrived(piece(at, 1 + h, k), near_sems[h, s, d])
+
+    to_near(z, 0, 1, 0)
+    layer_copy = pltpu.make_async_copy(layer_out, layer_hbm.at[0], local_sems.at[3])
 
     def gath_ready(o):
         if o == 1:
+            to_near(z, 1, 1, 0)
             to_core(z, 0, 1, 0)
             layer_out[...] = (hidden * gate).astype(BF)
+            layer_copy.start()
             w_term[...] = (
                 lax.dot_general(summed, hidden_grad, (((0,), (0,)), ((), ())), preferred_element_type=F32)
                 * (n_row * n_col * 128) ** (-0.5)
             ).reshape(w_term.shape)
-            arrived(gath_at(z, 1), near_sem)
+            from_near(z, 0, 1, 0)
+
+    def gath_block(at, o, s, d):
+        if o == 0 and d < HZ:
+            to_near(at, 1, s, d)
+        to_core(at, o, s, d)
+
+    last_sem = fresh()
 
     def backward_chunk(at):
         product = lax.dot_general(
@@ -265,8 +291,8 @@
         return product
 
     def accumulate(keys, at, start=False):
-        for o, s, d in keys:
-            arrived(gath_other(at, o), pair_sems[o, s, d])
+        for p, s, d in keys:
+            arrived(piece(at, p, 1 - k), pair_sems[p, s, d])
         if start:
             acc[...] = backward_chunk(at)
         else:
@@ -308,21 +334,35 @@
         for _ in range(count):
             next(weight_run, None)
 
-    gather_run = ring_gather(z, Z, gath_at, z_plus, z_minus, ready=gath_ready, on_block=to_core)
+    gather_run = ring_gather(
+        z, Z, lambda at, o: piece(at, o, k), z_plus, z_minus, ready=gath_ready, on_block=gath_block
+    )
     next(gather_run)
     to_core(z, 1, 1, 0)
     weight_step(1)
-    accumulate([(0, 1, 0), (1, 1, 0)], z, start=True)
+    from_near(z, 1, 1, 0)
+    to_core(z, 2, 1, 0)
     weight_step(1)
     for d in range(1, HZ + 1):
         next(gather_run, None)
         weight_step(2)
+        if d == 1:
+            accumulate([(p, 1, 0) for p in range(3)], z, start=True)
+        else:
+            for s in (1, -1):
+                accumulate([(p, s, d - 1) for p in range(3)], (z - s * (d - 1) + Z) % Z)
+        weight_step(2)
         if d < HZ:
-            for s in (1, -1):
-                accumulate([(0, s, d), (1, s, d)], (z - s * d + Z) % Z)
-        else:
-            accumulate([(0, 1, d), (1, -1, d)], (z + HZ) % Z)
-        weight_step(2)
+            for s in (-1, 1):
+                at = (z - s * d + Z) % Z
+                from_near(at, 1, s, d)
+                if d == HZ - 1 and s == -1:
+                    send(piece(at, 2, k), piece(at, 2, k), last_sem, z_minus)
+                to_core(at, 2, s, d)
+    far = (z + HZ) % Z
+    arrived(piece(far, 2, k), last_sem)
+    to_core(far, 2, -1, HZ)
+    accumulate([(0, 1, HZ), (1, -1, HZ), (2, -1, HZ)], far)
 
     back[...] = acc[...].astype(BF).reshape(back.shape)
 
@@ -344,12 +384,27 @@
     mine = total(0)
     for _ in weight_run:
         pass
-    weight_grad[...] = w_x[...].reshape(weight_grad.shape)
+    weight_grad_copy = pltpu.make_async_copy(w_x, weight_grad_hbm.reshape(w_x.shape), local_sems.at[4])
+    weight_grad_copy.start()
     arrived(xb_in, far_back)
     feat_grad[...] = (mine + xb_in[...].astype(F32)).astype(BF)
+    feat_grad_copy = pltpu.make_async_copy(feat_grad, feat_grad_hbm.at[0], local_sems.at[5])
+    feat_grad_copy.start()
     for copy in pending:
         copy.wait_send()
+    layer_copy.wait()
+    weight_grad_copy.wait()
+    feat_grad_copy.wait()
     assert counters["send"] <= send_sems.shape[0] and counters["recv"] <= recv_sems.shape[0]
+
+
+def write_outputs(layer_out, feat_grad, weight_grad, layer_hbm, feat_grad_hbm, weight_grad_hbm, sems):
+    pairs = ((weight_grad, weight_grad_hbm), (feat_grad, feat_grad_hbm), (layer_out, layer_hbm))
+    copies = [pltpu.make_async_copy(src, dst, sems.at[i]) for i, (src, dst) in enumerate(pairs)]
+    for copy in copies:
+        copy.start()
+    for copy in copies:
+        copy.wait()
 
 
 def local(n_row, n_col, feats, weight, cotangent, tile_values, tile_rows, tile_cols, tile_count):
@@ -362,11 +417,16 @@
     ids = jnp.where(slot_ids < tile_count[0, 0], ids, -1)
     places = jnp.arange(row_tiles * col_tiles, dtype=jnp.int32)
     hit = ids[None, :] == places[:, None]
-    tab = jnp.min(jnp.where(hit, slot_ids[None, :], slots), axis=1).reshape(row_tiles, col_tiles)
+    tab = jnp.min(jnp.where(hit, slot_ids[None, :], slots), axis=1)
 
     block = (128, width)
     w_rows = width // (CORE * Y * X)
+    w_full = (CORE, Y, X, 2, w_rows // 2, width)
     scratch = [
+        pltpu.VMEM((width, width), BF),
+        pltpu.VMEM(block, BF),
+        pltpu.VMEM(block, BF),
+        pltpu.VMEM(block, BF),
         pltpu.VMEM((slots + 1, 128, 128), BF),
         pltpu.VMEM((row_tiles * 128, col_tiles * 128), BF),
         pltpu.VMEM((n_row,) + block, BF),
@@ -389,33 +449,41 @@
         pltpu.VMEM((2, X // 2, 2, w_rows // 2, width), F32),
         pltpu.VMEM((X // 2, 2, w_rows // 2, width), F32),
         pltpu.VMEM((X // 2, 2, w_rows // 2, width), F32),
-        pltpu.VMEM((CORE, Y, X, 2, w_rows // 2, width), F32),
+        pltpu.VMEM(w_full, F32),
         pltpu.VMEM((Z, 2, w_rows // 2, width), F32),
         pltpu.SemaphoreType.DMA,
-        pltpu.SemaphoreType.DMA((140,)),
-        pltpu.SemaphoreType.DMA((170,)),
+        pltpu.SemaphoreType.DMA((6,)),
+        pltpu.SemaphoreType.DMA((180,)),
+        pltpu.SemaphoreType.DMA((210,)),
         pltpu.SemaphoreType.DMA((Z,)),
         pltpu.SemaphoreType.DMA((Z,)),
     ]
-    vmem = pl.BlockSpec(memory_space=pltpu.VMEM)
+    hbm = pl.BlockSpec(memory_space=pltpu.HBM)
     layer_out, feat_grad, weight_grad = pl.pallas_call(
         functools.partial(layer_kernel, n_row, n_col),
         out_shape=(
-            jax.ShapeDtypeStruct(block, BF),
-            jax.ShapeDtypeStruct(block, BF),
+            jax.ShapeDtypeStruct((1,) + block, BF),
+            jax.ShapeDtypeStruct((1,) + block, BF),
             jax.ShapeDtypeStruct((width, width), F32),
         ),
-        in_specs=[
-            pl.BlockSpec(memory_space=pltpu.SMEM), vmem, vmem, vmem,
-            pl.BlockSpec(memory_space=pl.ANY),
-        ],
-        out_specs=(vmem, vmem, vmem),
+        in_specs=[pl.BlockSpec(memory_space=pltpu.SMEM), hbm, hbm, hbm, hbm],
+        out_specs=(hbm, hbm, hbm),
         scratch_shapes=scratch,
         compiler_params=pltpu.CompilerParams(
             collective_id=0, has_side_effects=True, vmem_limit_bytes=60 * 1024 * 1024
         ),
-    )(tab, feats[0], weight, cotangent[0], tile_values[0, 0])
-    return layer_out[None], feat_grad[None], weight_grad
+    )(tab, feats, weight, cotangent, tile_values)
+    return pl.pallas_call(
+        write_outputs,
+        out_shape=(
+            jax.ShapeDtypeStruct((1,) + block, BF),
+            jax.ShapeDtypeStruct((1,) + block, BF),
+            jax.ShapeDtypeStruct((width, width), F32),
+        ),
+        in_specs=[hbm, hbm, hbm],
+        out_specs=(hbm, hbm, hbm),
+        scratch_shapes=[pltpu.SemaphoreType.DMA((3,))],
+    )(layer_out, feat_grad, weight_grad)
 
 
 def solution(mesh):

time: 132 us -> 169 us (1.28)
  Pallas kernels: 124 us -> 167 us
  local copies, waits for them, and re-layouts: 6.1 us -> 0 us
    pallas_call x0 -> x1, Pallas kernels: none -> 40.8 us  [local(): pl.pallas_call(write_outputs, out_shape=(jax.ShapeDtypeStruct((1,) + bloc...]
    unnamed x3 -> x0, local copies, waits for them, and re-layouts: 5.4 us -> none
    pallas_call x1, Pallas kernels: 124 us -> 126 us  [local(): pl.pallas_call(functools.partial(layer_kernel, n_row, n_col), out_shape=(...]
where the time goes in v2:
time: 169 us
  Pallas kernels  167 us (99%)
    pallas_call x1, Pallas kernels, local(): pl.pallas_call(functools.partial(layer_kernel, n_row, n_col), out_shape=(...  126 us
    pallas_call x1, Pallas kernels, local(): pl.pallas_call(write_outputs, out_shape=(jax.ShapeDtypeStruct((1,) + bloc...  40.8 us

profile of v2, /device:TPU:1, one launch (start us, length us, event | category | flops | bytes accessed | tf_op | source)
XLA Modules:
  0.0 169.3 jit_solution(15588207396821439140)
XLA Ops:
  1.3 0.7 compare_select_fusion
  2.0 0.7 select_reduce_fusion.tab
  2.6 125.9 %shard_map.94 = (bf16[1,128,512]{2,1,0:T(8,128)(2,1)}, bf16[1,128,512]{2,1,0:T(8,128)(2,1)}, f32[512,512]{1,0:T(8,128)}) custom-call(s32[256]{0:T(256)} %select_reduce_fusion.tab, bf16[1,128,512]{2,1,0:T(8,128)(2,1)} %feats_hbm.1, bf16[512,512]{1,0:T(8,128)(2,1)} %weight_hbm.1, bf16[1,128,512]{2,1,0:T(8,128)(2,1)} %cot_hbm.1, ...), custom_call_target="tpu_custom_call" | custom-call | tf_op jit(solution)/shard_map/pallas_call | solution.py:462
  128.5 40.8 %shard_map.95 = (bf16[1,128,512]{2,1,0:T(8,128)(2,1)}, bf16[1,128,512]{2,1,0:T(8,128)(2,1)}, f32[512,512]{1,0:T(8,128)}) custom-call(bf16[1,128,512]{2,1,0:T(8,128)(2,1)} %get-tuple-element.6.layer_out, bf16[1,128,512]{2,1,0:T(8,128)(2,1)} %get-tuple-element.7.feat_grad, f32[512,512]{1,0:T(8,128)} %get-tuple-element.8.weight_grad), custom_call_target="tpu_custom_call" | custom-call | tf_op jit(solution)/shard_map/pallas_call | solution.py:476

commit v3 on v2

--- a/solution.py
+++ b/solution.py
@@ -345,13 +345,13 @@
     weight_step(1)
     for d in range(1, HZ + 1):
         next(gather_run, None)
-        weight_step(2)
+        weight_step(1)
         if d == 1:
             accumulate([(p, 1, 0) for p in range(3)], z, start=True)
         else:
             for s in (1, -1):
                 accumulate([(p, s, d - 1) for p in range(3)], (z - s * (d - 1) + Z) % Z)
-        weight_step(2)
+        weight_step(1)
         if d < HZ:
             for s in (-1, 1):
                 at = (z - s * d + Z) % Z
@@ -398,13 +398,23 @@
     assert counters["send"] <= send_sems.shape[0] and counters["recv"] <= recv_sems.shape[0]
 
 
-def write_outputs(layer_out, feat_grad, weight_grad, layer_hbm, feat_grad_hbm, weight_grad_hbm, sems):
-    pairs = ((weight_grad, weight_grad_hbm), (feat_grad, feat_grad_hbm), (layer_out, layer_hbm))
-    copies = [pltpu.make_async_copy(src, dst, sems.at[i]) for i, (src, dst) in enumerate(pairs)]
-    for copy in copies:
-        copy.start()
-    for copy in copies:
-        copy.wait()
+def write_outputs(
+    layer_out, feat_grad, weight_grad, layer_hbm, feat_grad_hbm, weight_grad_hbm, layer_buf, feat_grad_buf, weight_buf, sems
+):
+    rows = weight_buf.shape[0] // 4
+    jobs = [(feat_grad, feat_grad_buf, feat_grad_hbm), (layer_out, layer_buf, layer_hbm)]
+    for i in range(4):
+        at = pl.ds(i * rows, rows)
+        jobs.append((weight_grad.at[at], weight_buf.at[at], weight_grad_hbm.at[at]))
+    reads = [pltpu.make_async_copy(src, buf, sems.at[0, i]) for i, (src, buf, _) in enumerate(jobs)]
+    writes = [pltpu.make_async_copy(buf, dst, sems.at[1, i]) for i, (_, buf, dst) in enumerate(jobs)]
+    for read in reads:
+        read.start()
+    for read, write in zip(reads, writes):
+        read.wait()
+        write.start()
+    for write in writes:
+        write.wait()
 
 
 def local(n_row, n_col, feats, weight, cotangent, tile_values, tile_rows, tile_cols, tile_count):
@@ -482,7 +492,12 @@
         ),
         in_specs=[hbm, hbm, hbm],
         out_specs=(hbm, hbm, hbm),
-        scratch_shapes=[pltpu.SemaphoreType.DMA((3,))],
+        scratch_shapes=[
+            pltpu.VMEM((1,) + block, BF),
+            pltpu.VMEM((1,) + block, BF),
+            pltpu.VMEM((width, width), F32),
+            pltpu.SemaphoreType.DMA((2, 6)),
+        ],
     )(layer_out, feat_grad, weight_grad)
 
 

time: 169 us -> 116 us (0.69)
  Pallas kernels: 167 us -> 113 us
    pallas_call x1, Pallas kernels: 40.8 us -> 2.15 us  [local(): pl.pallas_call(write_outputs, out_shape=(jax.ShapeDtypeStruct((1,) + bloc...]
    pallas_call x1, Pallas kernels: 126 us -> 111 us  [local(): pl.pallas_call(functools.partial(layer_kernel, n_row, n_col), out_shape=(...]
where the time goes in v3:
time: 116 us
  Pallas kernels  113 us (97%)
  other arithmetic  1.34 us (1%)
  between operations  1.29 us (1%)
    pallas_call x1, Pallas kernels, local(): pl.pallas_call(functools.partial(layer_kernel, n_row, n_col), out_shape=(...  111 us

profile of v3, /device:TPU:1, one launch (start us, length us, event | category | flops | bytes accessed | tf_op | source)
XLA Modules:
  0.0 115.7 jit_solution(5887842292675045473)
XLA Ops:
  1.3 0.7 compare_select_fusion
  2.0 0.7 select_reduce_fusion.tab
  2.6 111.0 %shard_map.94 = (bf16[1,128,512]{2,1,0:T(8,128)(2,1)}, bf16[1,128,512]{2,1,0:T(8,128)(2,1)}, f32[512,512]{1,0:T(8,128)}) custom-call(s32[256]{0:T(256)} %select_reduce_fusion.tab, bf16[1,128,512]{2,1,0:T(8,128)(2,1)} %feats_hbm.1, bf16[512,512]{1,0:T(8,128)(2,1)} %weight_hbm.1, bf16[1,128,512]{2,1,0:T(8,128)(2,1)} %cot_hbm.1, ...), custom_call_target="tpu_custom_call" | custom-call | tf_op jit(solution)/shard_map/pallas_call | solution.py:472
  113.6 2.1 %shard_map.95 = (bf16[1,128,512]{2,1,0:T(8,128)(2,1)}, bf16[1,128,512]{2,1,0:T(8,128)(2,1)}, f32[512,512]{1,0:T(8,128)}) custom-call(bf16[1,128,512]{2,1,0:T(8,128)(2,1)} %get-tuple-element.6.layer_out, bf16[1,128,512]{2,1,0:T(8,128)(2,1)} %get-tuple-element.7.feat_grad, f32[512,512]{1,0:T(8,128)} %get-tuple-element.8.weight_grad), custom_call_target="tpu_custom_call" | custom-call | tf_op jit(solution)/shard_map/pallas_call | solution.py:486

commit v4 on v3

--- a/solution.py
+++ b/solution.py
@@ -93,7 +93,7 @@
                     if on_block is not None:
                         on_block(at, o, s, d)
 
-    def ring_sum(pos, n, view, bufs_p, bufs_m, plus, minus, before=None):
+    def ring_sum(pos, n, view, bufs_p, bufs_m, plus, minus, before=None, middle=None, defer=False):
         half = n // 2
         bufs, dev = {1: bufs_p, -1: bufs_m}, {1: plus, -1: minus}
         sems = {(s, d, o): fresh() for s in (1, -1) for d in range(half) for o in (0, 1)}
@@ -103,11 +103,18 @@
                 d = first[s, o]
                 if d > 0 and d == half:
                     send(view((pos + s * d + n) % n, o), bufs[s].at[d - 1, o], sems[s, d - 1, o], dev[s])
+        if middle is not None:
+            middle()
+
+        def second(s, o):
+            d = first[s, o]
+            if d > 0 and d < half:
+                send(view((pos + s * d + n) % n, o), bufs[s].at[d - 1, o], sems[s, d - 1, o], dev[s])
+
         for o in (1, 0):
             for s in (1, -1):
-                d = first[s, o]
-                if d > 0 and d < half:
-                    send(view((pos + s * d + n) % n, o), bufs[s].at[d - 1, o], sems[s, d - 1, o], dev[s])
+                if not (defer and (s, o) == (-1, 0)):
+                    second(s, o)
         for d in range(half - 1, 0, -1):
             yield
             if before is not None:
@@ -120,6 +127,8 @@
                     arrived(buf, sems[s, d, o])
                     add_into(buf, view((pos + s * d + n) % n, o))
                     send(buf, bufs[s].at[d - 1, o], sems[s, d - 1, o], dev[s])
+                    if defer and d == half - 1 and (s, o) == (-1, 1):
+                        second(-1, 0)
         yield
         if before is not None:
             before(0)
@@ -200,9 +209,13 @@
     def sum_at(at, o):
         return core_in.at[at, xl if o == 0 else 1 - xl]
 
-    lax.fori_loop(0, 3, forward_chunk, 0)
-    for t in range(3):
-        core_total(t)
+    lax.fori_loop(0, 2, forward_chunk, 0)
+    core_total(0)
+
+    def middle():
+        forward_chunk(2, 0)
+        core_total(1)
+        core_total(2)
 
     done = [3]
 
@@ -213,7 +226,7 @@
             core_total(done[0])
             done[0] += 1
 
-    steps = ring_sum(z, Z, sum_at, rp, rm, z_plus, z_minus, before=before)
+    steps = ring_sum(z, Z, sum_at, rp, rm, z_plus, z_minus, before=before, middle=middle)
     while True:
         try:
             next(steps)
@@ -369,7 +382,7 @@
     def back_at(at, o):
         return back.at[xh if o == 0 else 1 - xh, at]
 
-    steps = ring_sum(y, Y, back_at, yp, ym, y_plus, y_minus)
+    steps = ring_sum(y, Y, back_at, yp, ym, y_plus, y_minus, defer=True)
     while True:
         try:
             next(steps)

time: 116 us -> 117 us (level)
  no operation moved by 1% of the time
where the time goes in v4:
time: 117 us
  Pallas kernels  114 us (97%)
  other arithmetic  1.34 us (1%)
  between operations  1.29 us (1%)
    pallas_call x1, Pallas kernels, local(): pl.pallas_call(functools.partial(layer_kernel, n_row, n_col), out_shape=(...  112 us

profile of v4, /device:TPU:1, one launch (start us, length us, event | category | flops | bytes accessed | tf_op | source)
XLA Modules:
  0.0 116.6 jit_solution(7646699548415188771)
XLA Ops:
  1.3 0.7 compare_select_fusion
  2.0 0.7 select_reduce_fusion.tab
  2.6 111.8 %shard_map.94 = (bf16[1,128,512]{2,1,0:T(8,128)(2,1)}, bf16[1,128,512]{2,1,0:T(8,128)(2,1)}, f32[512,512]{1,0:T(8,128)}) custom-call(s32[256]{0:T(256)} %select_reduce_fusion.tab, bf16[1,128,512]{2,1,0:T(8,128)(2,1)} %feats_hbm.1, bf16[512,512]{1,0:T(8,128)(2,1)} %weight_hbm.1, bf16[1,128,512]{2,1,0:T(8,128)(2,1)} %cot_hbm.1, ...), custom_call_target="tpu_custom_call" | custom-call | tf_op jit(solution)/shard_map/pallas_call | solution.py:485
  114.4 2.1 %shard_map.95 = (bf16[1,128,512]{2,1,0:T(8,128)(2,1)}, bf16[1,128,512]{2,1,0:T(8,128)(2,1)}, f32[512,512]{1,0:T(8,128)}) custom-call(bf16[1,128,512]{2,1,0:T(8,128)(2,1)} %get-tuple-element.6.layer_out, bf16[1,128,512]{2,1,0:T(8,128)(2,1)} %get-tuple-element.7.feat_grad, f32[512,512]{1,0:T(8,128)} %get-tuple-element.8.weight_grad), custom_call_target="tpu_custom_call" | custom-call | tf_op jit(solution)/shard_map/pallas_call | solution.py:499

commit v5 on v3

--- a/solution.py
+++ b/solution.py
@@ -345,13 +345,11 @@
     weight_step(1)
     for d in range(1, HZ + 1):
         next(gather_run, None)
-        weight_step(1)
         if d == 1:
             accumulate([(p, 1, 0) for p in range(3)], z, start=True)
         else:
             for s in (1, -1):
                 accumulate([(p, s, d - 1) for p in range(3)], (z - s * (d - 1) + Z) % Z)
-        weight_step(1)
         if d < HZ:
             for s in (-1, 1):
                 at = (z - s * d + Z) % Z
@@ -359,6 +357,7 @@
                 if d == HZ - 1 and s == -1:
                     send(piece(at, 2, k), piece(at, 2, k), last_sem, z_minus)
                 to_core(at, 2, s, d)
+        weight_step(2)
     far = (z + HZ) % Z
     arrived(piece(far, 2, k), last_sem)
     to_core(far, 2, -1, HZ)

time: 116 us -> 120 us (1.034)
  Pallas kernels: 113 us -> 118 us
    pallas_call x1, Pallas kernels: 111 us -> 116 us  [local(): pl.pallas_call(functools.partial(layer_kernel, n_row, n_col), out_shape=(...]
where the time goes in v5:
time: 120 us
  Pallas kernels  118 us (98%)
  other arithmetic  1.34 us (1%)
  between operations  1.29 us (1%)
    pallas_call x1, Pallas kernels, local(): pl.pallas_call(functools.partial(layer_kernel, n_row, n_col), out_shape=(...  116 us

profile of v5, /device:TPU:1, one launch (start us, length us, event | category | flops | bytes accessed | tf_op | source)
XLA Modules:
  0.0 120.3 jit_solution(459849663364891284)
XLA Ops:
  1.3 0.7 compare_select_fusion
  2.0 0.7 select_reduce_fusion.tab
  2.6 115.5 %shard_map.94 = (bf16[1,128,512]{2,1,0:T(8,128)(2,1)}, bf16[1,128,512]{2,1,0:T(8,128)(2,1)}, f32[512,512]{1,0:T(8,128)}) custom-call(s32[256]{0:T(256)} %select_reduce_fusion.tab, bf16[1,128,512]{2,1,0:T(8,128)(2,1)} %feats_hbm.1, bf16[512,512]{1,0:T(8,128)(2,1)} %weight_hbm.1, bf16[1,128,512]{2,1,0:T(8,128)(2,1)} %cot_hbm.1, ...), custom_call_target="tpu_custom_call" | custom-call | tf_op jit(solution)/shard_map/pallas_call | solution.py:471
  118.1 2.1 %shard_map.95 = (bf16[1,128,512]{2,1,0:T(8,128)(2,1)}, bf16[1,128,512]{2,1,0:T(8,128)(2,1)}, f32[512,512]{1,0:T(8,128)}) custom-call(bf16[1,128,512]{2,1,0:T(8,128)(2,1)} %get-tuple-element.6.layer_out, bf16[1,128,512]{2,1,0:T(8,128)(2,1)} %get-tuple-element.7.feat_grad, f32[512,512]{1,0:T(8,128)} %get-tuple-element.8.weight_grad), custom_call_target="tpu_custom_call" | custom-call | tf_op jit(solution)/shard_map/pallas_call | solution.py:485
